TPU v7x, 128 devices: a whole 4x4x4 slice. The times are simulated.
128 devices in a mesh: grp: 8 (over z, core), tok: 16 (over y, x).
Axes of the slice: x: 4, y: 4, z: 4, core: 2. Of those that a mesh axis runs over, the one named last changes fastest.
Arguments:
- guess_symbol_ids: int32 [4096], replicated, may hold values from 0 to 32767
- symbol_vector_lookup: bfloat16 [32768, 4096], P('tok', 'grp'), may hold values from -6 to 6
- prior_attention_normed: bfloat16 [256, 4096], P('tok', 'grp'), may hold values from -6 to 6
- prior_feedforward_normed: bfloat16 [256, 4096], P('tok', 'grp'), may hold values from -6 to 6
- layernorm_scales: float32 [3, 4096], replicated, may hold values from 0.25 to 1.75
- lagged_blend_ratios: float32 [7, 4096], replicated, may hold values from 0.05 to 0.95
- attention_matrices: bfloat16 [4, 4096, 4096], P(None, None, 'grp'), may hold values from -0.09375 to 0.09375
- forgetting_baseline_vector: float32 [4096], replicated, may hold values from -6 to -0.5
- forgetting_narrow_matrix: bfloat16 [4096, 128], replicated, may hold values from -0.09375 to 0.09375
- forgetting_widen_matrix: bfloat16 [128, 4096], P(None, 'grp'), may hold values from -0.5 to 0.5
- diagonal_boost: float32 [4096], replicated, may hold values from -3 to 3
- attention_result_matrix: bfloat16 [4096, 4096], P('grp', 'tok'), may hold values from -0.09375 to 0.09375
- feedforward_lookup_matrix: bfloat16 [4096, 7168], P('tok', 'grp'), may hold values from -0.09375 to 0.09375
- feedforward_content_matrix: bfloat16 [7168, 4096], P('grp', 'tok'), may hold values from -0.0625 to 0.0625
- feedforward_gating_matrix: bfloat16 [4096, 4096], P('tok', 'grp'), may hold values from -0.09375 to 0.09375
- memory_matrix_store: float32 [256, 64, 4096], P('tok', 'grp'), may hold values from -6 to 6
- query_memory_slot: int32 [128], replicated, may hold values from 0 to 255, as said below
- candidate_tally_each_query: int32 [16, 8], replicated, may hold values from 1 to 4, 16 in all within a row
- kept_guess_tally: int32 [256], P('tok'), may hold values from 0 to 16
Outputs:
- layer_out: bfloat16 [4096, 4096], P('tok', 'grp')
- shift_att_out: bfloat16 [256, 4096], P('tok', 'grp')
- shift_ffn_out: bfloat16 [256, 4096], P('tok', 'grp')
- store_out: float32 [256, 64, 4096], P('tok', 'grp')
Inputs may be any that keep to these rules, and one draw needn't show every extreme that they name: `query_memory_slot`: pages of different requests differ. Page p lies on tok index p // 16, slot p % 16. The 8 requests r * 8 onward, whose branches are branches r * 16 onward, have pages on pairwise different tok indices. `candidate_tally_each_query`: row r holds the branch counts of requests r * 8 onward, in order; each row sums to 16.
All inputs are finite; a program needn't handle non-finite values.
Results may differ from a plain program's by a relative error of at most 0.02.
Values may be sent and summed in bfloat16 or wider, within the bound.
A program may use at most 192 MiB of HBM per device.

v0:
```python
import jax
import jax.numpy as jnp
from jax import lax
from jax.sharding import PartitionSpec as P

HIDDEN_BREADTH = 4096
PART_BREADTH = 64
GUESS_SYMBOLS = 16
EPSILON = 1e-05
HEAD_EPSILON = 0.00064


def normalize(tensor, gain_row, eps_value):
    row_mean = jnp.mean(tensor, axis=-1, keepdims=True)
    centered = tensor - row_mean
    spread = jnp.mean(centered * centered, axis=-1, keepdims=True)
    return centered * lax.rsqrt(spread + eps_value) * gain_row


def shifted(normed, carried):
    return jnp.concatenate([carried.astype(jnp.float32)[:, None, :], normed[:, :-1, :]], axis=1)


def mix_input(normed, before, coeff):
    return (normed + (before - normed) * coeff).reshape(-1, normed.shape[-1]).astype(jnp.bfloat16)


def memory_matrix_sweep(
    gating_vectors,
    lookup_vectors,
    content_vectors,
    forgetting_multiplier,
    extra_head_rows,
    initial_memory_matrix,
    accepted_count,
    draft_length,
):

    def scan_step(carry_state, inputs):
        wkv_state, chosen_candidate = carry_state
        current_receptance, current_key, current_value, decay_now, step_index = inputs
        current_token_term = (
            jnp.sum(current_receptance * extra_head_rows * current_key, axis=-1, keepdims=True)
            * current_value
        )
        head_out = (
            jnp.einsum(
                "bhi,bhij->bhj", current_receptance, wkv_state, precision=lax.Precision.HIGHEST
            )
            + current_token_term
        )
        wkv_state = (
            decay_now[..., None] * wkv_state + current_key[..., None] * current_value[..., None, :]
        )
        chosen_candidate = jnp.where(
            (accepted_count == step_index + 1)[:, None, None, None], wkv_state, chosen_candidate
        )
        return ((wkv_state, chosen_candidate), head_out)

    step_ids = jnp.arange(draft_length, dtype=jnp.int32)
    (final_state, chosen_candidate), attention_part_results = lax.scan(
        scan_step,
        (initial_memory_matrix, initial_memory_matrix),
        (gating_vectors, lookup_vectors, content_vectors, forgetting_multiplier, step_ids),
    )
    return (attention_part_results, chosen_candidate)


def keep_shift(normed, carried, kept_guess_tally, first_vector_slice, hidden_breadth):
    last_index = jnp.maximum(kept_guess_tally - 1, 0)
    picked = jnp.take_along_axis(normed, last_index[:, None, None], axis=1)[:, 0]
    picked = lax.dynamic_slice_in_dim(picked, first_vector_slice, hidden_breadth, 1)
    return jnp.where((kept_guess_tally > 0)[:, None], picked, carried.astype(jnp.float32)).astype(
        jnp.bfloat16
    )


def add_rows(operand, piece):
    return jnp.dot(operand, piece, preferred_element_type=jnp.float32)


def body(
    guess_symbol_ids,
    symbol_vector_lookup,
    prior_attention_normed,
    prior_feedforward_normed,
    layernorm_scales,
    lagged_blend_ratios,
    attention_matrices,
    forgetting_baseline_vector,
    forgetting_narrow_matrix,
    forgetting_widen_matrix,
    diagonal_boost,
    attention_result_matrix,
    feedforward_lookup_matrix,
    feedforward_content_matrix,
    feedforward_gating_matrix,
    memory_matrix_store,
    query_memory_slot,
    candidate_tally_each_query,
    kept_guess_tally,
):
    tok_count = lax.axis_size("tok")
    tok_at = lax.axis_index("tok")
    grp_at = lax.axis_index("grp")
    branch_local, hidden_breadth = prior_attention_normed.shape
    row_count = branch_local * GUESS_SYMBOLS
    vocab_rows = symbol_vector_lookup.shape[0]
    first_vector_slice = grp_at * hidden_breadth
    head_local_output = hidden_breadth // PART_BREADTH
    wanted = guess_symbol_ids - tok_at * vocab_rows
    inside = (wanted >= 0) & (wanted < vocab_rows)
    found = jnp.take(symbol_vector_lookup, jnp.clip(wanted, 0, vocab_rows - 1), axis=0)
    embedded = lax.psum_scatter(
        jnp.where(inside[:, None], found.astype(jnp.float32), 0.0).astype(jnp.bfloat16),
        "tok",
        scatter_dimension=0,
        tiled=True,
    )
    whole_x, whole_att, whole_ffn = (
        lax.all_gather(embedded, "grp", axis=1, tiled=True),
        lax.all_gather(prior_attention_normed, "grp", axis=1, tiled=True),
        lax.all_gather(prior_feedforward_normed, "grp", axis=1, tiled=True),
    )
    base_values = whole_x.astype(jnp.float32)
    normed = normalize(base_values, layernorm_scales[0], EPSILON).reshape(
        branch_local, GUESS_SYMBOLS, HIDDEN_BREADTH
    )
    before = shifted(normed, whole_att)

    def project(index, weight):
        return jnp.dot(
            mix_input(normed, before, lagged_blend_ratios[index]),
            weight,
            preferred_element_type=jnp.float32,
        )

    gating_vectors = project(0, attention_matrices[0])
    lookup_vectors = project(1, attention_matrices[1])
    content_vectors = project(2, attention_matrices[2])
    gate_proj = jax.nn.silu(project(3, attention_matrices[3]))
    lowrank = jnp.tanh(project(4, forgetting_narrow_matrix)).astype(jnp.bfloat16)
    base_decay = lax.dynamic_slice_in_dim(
        forgetting_baseline_vector, first_vector_slice, hidden_breadth, 0
    )
    forgetting_multiplier = jnp.exp(
        -jnp.exp(
            base_decay
            + jnp.dot(lowrank, forgetting_widen_matrix, preferred_element_type=jnp.float32)
        )
    )
    slot_count = memory_matrix_store.shape[0]
    req_local = candidate_tally_each_query.shape[1]
    owners = (query_memory_slot // slot_count).reshape(tok_count, req_local)
    places = (query_memory_slot % slot_count).reshape(tok_count, req_local)
    owned_here = owners == tok_at
    send_slot = jnp.sum(jnp.where(owned_here, places, 0), axis=1)
    sending = jnp.any(owned_here, axis=1)
    outgoing = jnp.where(
        sending[:, None, None], jnp.take(memory_matrix_store, send_slot, axis=0), 0.0
    )
    incoming = lax.all_to_all(
        outgoing.astype(jnp.bfloat16), "tok", split_axis=0, concat_axis=0, tiled=True
    ).astype(outgoing.dtype)
    my_owners = lax.dynamic_index_in_dim(owners, tok_at, 0, keepdims=False)
    my_pages = jnp.take(incoming, my_owners, axis=0)
    my_counts = lax.dynamic_index_in_dim(candidate_tally_each_query, tok_at, 0, keepdims=False)
    request_ends = jnp.cumsum(my_counts)
    local_ids = jnp.arange(branch_local, dtype=jnp.int32)
    request_of = jnp.sum((request_ends[None, :] <= local_ids[:, None]).astype(jnp.int32), axis=1)
    initial_memory_matrix = jnp.take(my_pages, request_of, axis=0).reshape(
        branch_local, head_local_output, PART_BREADTH, PART_BREADTH
    )

    def divide_among_parts(tensor):
        return tensor.reshape(
            branch_local, GUESS_SYMBOLS, head_local_output, PART_BREADTH
        ).transpose(1, 0, 2, 3)

    surplus_nearby_entries = lax.dynamic_slice_in_dim(
        diagonal_boost, first_vector_slice, hidden_breadth, 0
    ).reshape(head_local_output, PART_BREADTH)
    attention_part_results, chosen_candidate = memory_matrix_sweep(
        divide_among_parts(gating_vectors),
        divide_among_parts(lookup_vectors),
        divide_among_parts(content_vectors),
        divide_among_parts(forgetting_multiplier),
        surplus_nearby_entries,
        initial_memory_matrix,
        kept_guess_tally,
        GUESS_SYMBOLS,
    )
    head_gain = lax.dynamic_slice_in_dim(
        layernorm_scales[2], first_vector_slice, hidden_breadth, 0
    ).reshape(head_local_output, PART_BREADTH)
    head_normed = (
        normalize(attention_part_results, head_gain, HEAD_EPSILON)
        .transpose(1, 0, 2, 3)
        .reshape(row_count, hidden_breadth)
    )
    attended = (head_normed * gate_proj).astype(jnp.bfloat16)
    partial_att = jnp.dot(
        attended,
        lax.all_gather(attention_result_matrix, "tok", axis=1, tiled=True),
        preferred_element_type=jnp.float32,
    )
    shares = lax.psum_scatter(
        partial_att.astype(jnp.bfloat16), "grp", scatter_dimension=1, tiled=True
    ).astype(jnp.float32)
    own_x = lax.dynamic_slice_in_dim(base_values, first_vector_slice, hidden_breadth, 1)
    residual = (own_x + shares).astype(jnp.bfloat16)
    whole_res = lax.all_gather(residual, "grp", axis=1, tiled=True)
    residual_values = whole_res.astype(jnp.float32)
    normed2 = normalize(residual_values, layernorm_scales[1], EPSILON).reshape(
        branch_local, GUESS_SYMBOLS, HIDDEN_BREADTH
    )
    before2 = shifted(normed2, whole_ffn)
    key_in = mix_input(normed2, before2, lagged_blend_ratios[5])
    rec_in = mix_input(normed2, before2, lagged_blend_ratios[6])
    key_sum = add_rows(key_in, lax.all_gather(feedforward_lookup_matrix, "tok", axis=0, tiled=True))
    rec_sum = add_rows(rec_in, lax.all_gather(feedforward_gating_matrix, "tok", axis=0, tiled=True))
    hidden = jnp.square(jax.nn.relu(key_sum)).astype(jnp.bfloat16)
    partial_ffn = jnp.dot(
        hidden,
        lax.all_gather(feedforward_content_matrix, "tok", axis=1, tiled=True),
        preferred_element_type=jnp.float32,
    )
    ffn_share = lax.psum_scatter(
        partial_ffn.astype(jnp.bfloat16), "grp", scatter_dimension=1, tiled=True
    ).astype(jnp.float32)
    layer_out = (residual.astype(jnp.float32) + jax.nn.sigmoid(rec_sum) * ffn_share).astype(
        jnp.bfloat16
    )
    shift_att_out = keep_shift(
        normed, prior_attention_normed, kept_guess_tally, first_vector_slice, hidden_breadth
    )
    shift_ffn_out = keep_shift(
        normed2, prior_feedforward_normed, kept_guess_tally, first_vector_slice, hidden_breadth
    )
    branch_score = kept_guess_tally * branch_local + (branch_local - 1 - local_ids)
    member = request_of[None, :] == jnp.arange(req_local, dtype=jnp.int32)[:, None]
    best_score = jnp.max(jnp.where(member, branch_score[None, :], -1), axis=1)
    winner = branch_local - 1 - best_score % branch_local
    new_pages = jnp.take(chosen_candidate, winner, axis=0).reshape(
        req_local, head_local_output, PART_BREADTH * PART_BREADTH
    )
    targets = my_owners[None, :] == jnp.arange(tok_count, dtype=jnp.int32)[:, None]
    pick_index = jnp.sum(
        jnp.where(targets, jnp.arange(req_local, dtype=jnp.int32)[None, :], 0), axis=1
    )
    going = jnp.any(targets, axis=1)
    outgoing_back = jnp.where(going[:, None, None], jnp.take(new_pages, pick_index, axis=0), 0.0)
    returned = lax.all_to_all(
        outgoing_back.astype(jnp.bfloat16), "tok", split_axis=0, concat_axis=0, tiled=True
    ).astype(outgoing_back.dtype)
    writes = (
        (send_slot[None, :] == jnp.arange(slot_count, dtype=jnp.int32)[:, None]) & sending[None, :]
    ).astype(jnp.float32)
    placed = jnp.dot(
        writes, returned.reshape(tok_count, -1), precision=lax.Precision.HIGHEST
    ).reshape(memory_matrix_store.shape)
    store_out = jnp.where(
        (jnp.sum(writes, axis=1) > 0.5)[:, None, None], placed, memory_matrix_store
    )
    return (layer_out, shift_att_out, shift_ffn_out, store_out)


def solution(mesh):
    in_specs = (
        P(),
        P("tok", "grp"),
        P("tok", "grp"),
        P("tok", "grp"),
        P(),
        P(),
        P(None, None, "grp"),
        P(),
        P(),
        P(None, "grp"),
        P(),
        P("grp", "tok"),
        P("tok", "grp"),
        P("grp", "tok"),
        P("tok", "grp"),
        P("tok", "grp", None),
        P(),
        P(),
        P("tok"),
    )
    out_specs = (P("tok", "grp"), P("tok", "grp"), P("tok", "grp"), P("tok", "grp", None))
    return jax.shard_map(body, mesh=mesh, in_specs=in_specs, out_specs=out_specs, check_vma=False)
```

profile of v0, /device:TPU:0, one launch (start us, length us, event | category | flops | bytes accessed | tf_op | source)
XLA Modules:
  0.0 823.8 jit_solution(9953232027514825805)
XLA Ops:
  8.9 17.3 %gather_fusion = bf16[4096,512]{1,0:T(8,128)(2,1)} fusion(bf16[2048,512]{1,0:T(8,128)(2,1)S(1)} %copy-done, s32[4096]{0:T(1024)S(1)} %fusion.51), kind=kCustom, calls=%fused_computation.4 | custom fusion | bytes 8404992 | tf_op jit(solution)/shard_map/jit(_take)/gather | solution.py:113
  26.2 5.3 select_convert_fusion
  31.5 80.0 %reduce-scatter.4.cloned.1.call-done = bf16[256,512]{1,0:T(8,128)(2,1)} async-done(((bf16[4096,512]{1,0:T(8,128)(2,1)}), bf16[256,512]{1,0:T(8,128)(2,1)}) %reduce-scatter.4.cloned.1.call-update) | async-done | bytes 262160 | tf_op jit(solution)/shard_map/reduce_scatter | solution.py:114
  114.6 5.0 all-to-all-start
  120.5 13.3 %all_gather.25 = bf16[16,4096]{1,0:T(8,128)(2,1)S(1)} all-gather(bf16[16,512]{1,0:T(8,128)(2,1)S(1)} %copy-done.16), channel_id=1, replica_groups=mesh['grp'=8,'tok'=16] {'grp'}, dimensions={1}, use_global_device_ids=true | all-gather | bytes 147456 | tf_op jit(solution)/shard_map/all_gather | solution.py:122
  134.7 9.2 %slice_bitcast_fusion = (bf16[512,4096]{0,1:T(8,128)(2,1)}, bf16[512,4096]{0,1:T(8,128)(2,1)}, bf16[512,4096]{0,1:T(8,128)(2,1)}) fusion(bf16[4,4096,512]{2,1,0:T(8,128)(2,1)} %param.31), kind=kLoop, calls=%fused_computation.44 | loop fusion | bytes 25165824 | tf_op jit(solution)/shard_map/dot_general | solution.py:132
  143.9 6.4 copy.47
  150.3 6.4 copy.46
  156.8 6.5 copy.45
  174.5 3.1 reshape.315
  177.6 2.7 convert.9
  187.7 5.6 add_convert_fusion.3
  193.3 5.3 fusion.29
  203.2 6.3 convolution_bitcast_fusion
  209.6 3.3 convolution_bitcast_fusion.1
  212.9 3.3 convolution_bitcast_fusion.2
  216.3 284.8 %while.14 = (s32[]{:T(128)}, f32[16,8,64,64]{3,2,1,0:T(8,128)}, bf16[16,8,64,64]{3,2,1,0:T(8,128)(2,1)S(1)}, f32[16,16,8,64]{3,2,1,0:T(8,128)S(1)}, f32[16,16,8,...) while((s32[]{:T(128)}, f32[16,8,64,64]{3,2,1,0:T(8,128)}, ...), condition=%wide.region_9.11_spmd, body=%wide.region_7.10_spmd.sunk | while | flops 8421586 | bytes 9150729 | solution.py:61
  217.6 5.3 fusion.91
  227.5 6.6 broadcast_select_fusion.5
  235.3 5.3 fusion.91
  245.3 6.6 broadcast_select_fusion.5
  253.1 5.3 fusion.91
  263.1 6.6 broadcast_select_fusion.5
  270.9 5.3 fusion.91
  280.8 6.6 broadcast_select_fusion.5
  288.7 5.3 fusion.91
  298.6 6.6 broadcast_select_fusion.5
  306.5 5.3 fusion.91
  316.4 6.6 broadcast_select_fusion.5
  324.3 5.3 fusion.91
  334.2 6.6 broadcast_select_fusion.5
  342.1 5.3 fusion.91
  352.0 6.6 broadcast_select_fusion.5
  359.9 5.3 fusion.91
  369.8 6.6 broadcast_select_fusion.5
  377.7 5.3 fusion.91
  387.6 6.6 broadcast_select_fusion.5
  395.5 5.3 fusion.91
  405.4 6.6 broadcast_select_fusion.5
  413.3 5.3 fusion.91
  423.2 6.6 broadcast_select_fusion.5
  431.1 5.3 fusion.91
  441.0 6.6 broadcast_select_fusion.5
  448.8 5.3 fusion.91
  458.8 6.6 broadcast_select_fusion.5
  466.6 5.3 fusion.91
  476.6 6.6 broadcast_select_fusion.5
  484.4 5.3 fusion.91
  494.3 6.6 broadcast_select_fusion.5
  504.0 9.2 %convolution_convert_fusion.1 = bf16[256,4096]{1,0:T(8,128)(2,1)} fusion(bf16[512,4096]{1,0:T(8,128)(2,1)} %all-gather.9.cloned.1.call-done, f32[256,512]{1,0:T(8,128)} %reshape.318, bf16[4,4096,512]{2,1,0:T(8,128)(2,1)} %param.31, f32[256,4096]{1,0:T(8,128)} %get-tuple-element.145, f32[4096]{0:T(1024)S(1)} %bitcast.225, ...), kind=kOutput, calls=%fused_computation.28 | convolution fusion | flops 2156658688 | bytes 17336320 | tf_op jit(solution)/shard_map/dot_general | solution.py:202
  513.3 4.0 convert_element_type.95
  517.4 30.8 %reduce-scatter.6.cloned.1.call-done = bf16[256,512]{1,0:T(8,128)(2,1)} async-done(((bf16[256,4096]{1,0:T(8,128)(2,1)}), bf16[256,512]{1,0:T(8,128)(2,1)}) %reduce-scatter.6.cloned.1.call-update) | async-done | bytes 262160 | tf_op jit(solution)/shard_map/reduce_scatter | solution.py:207
  552.2 12.8 %all_gather.28 = bf16[16,4096]{1,0:T(8,128)(2,1)S(1)} all-gather(bf16[16,512]{1,0:T(8,128)(2,1)S(1)} %copy-done.18), channel_id=1, replica_groups=mesh['grp'=8,'tok'=16] {'grp'}, dimensions={1}, use_global_device_ids=true | all-gather | bytes 147456 | tf_op jit(solution)/shard_map/all_gather | solution.py:123
  565.4 9.2 %all-gather.11.cloned.1.call-done = bf16[256,4096]{1,0:T(8,128)(2,1)} async-done(((bf16[256,512]{1,0:T(8,128)(2,1)}), bf16[256,4096]{1,0:T(8,128)(2,1)}) %all-gather.11.cloned.1.call-update) | async-done | bytes 2097168 | tf_op jit(solution)/shard_map/all_gather | solution.py:212
  581.9 3.2 bitcast_subtract_fusion
  585.1 58.0 %all-gather.15.cloned.1.call-done = bf16[4096,896]{1,0:T(8,128)(2,1)} async-done(((bf16[256,896]{1,0:T(8,128)(2,1)}), bf16[4096,896]{1,0:T(8,128)(2,1)}) %all-gather.15.cloned.1.call-update) | async-done | bytes 7340048 | tf_op jit(solution)/shard_map/all_gather | solution.py:220
  643.1 75.0 %all-gather.17.cloned.1.call-done = bf16[896,4096]{1,0:T(8,128)(2,1)} async-done(((bf16[896,256]{1,0:T(8,128)(2,1)}), bf16[896,4096]{1,0:T(8,128)(2,1)}) %all-gather.17.cloned.1.call-update) | async-done | bytes 7340048 | tf_op jit(solution)/shard_map/all_gather | solution.py:225
  718.1 12.9 %convolution_convert_fusion = bf16[256,4096]{1,0:T(8,128)(2,1)} fusion(bf16[896,4096]{1,0:T(8,128)(2,1)} %all-gather.17.cloned.1.call-done, bf16[4096,896]{1,0:T(8,128)(2,1)} %all-gather.15.cloned.1.call-done, f32[256,4096]{1,0:T(8,128)} %bitcast_subtract_fusion, f32[4096]{0:T(1024)S(1)} %bitcast.224, bf16[256,4096]{1,0:T(8,128)(2,1)} %all-gather.11.cloned.1.call-done, ...), kind=kOutput, calls=%fused_computation.27 | convolution fusion | flops 3767173120 | bytes 23103488 | tf_op jit(solution)/shard_map/dot_general | solution.py:223
  734.9 5.2 all-to-all-start.1
  743.0 13.5 %all-to-all-done.1 = bf16[16,8,4096]{2,1,0:T(8,128)(2,1)S(1)} async-done(((bf16[16,8,4096]{2,1,0:T(8,128)(2,1)}), bf16[16,8,4096]{2,1,0:T(8,128)(2,1)S(1)}, u32[]{:S(2)}, u32[]{:S(2)}) %all-to-all-start.1) | async-done | bytes 1048608 | tf_op jit(solution)/shard_map/all_to_all | solution.py:253
  756.6 4.0 convolution_select_fusion
  765.6 9.0 %all-gather.13.cloned.1.call-done = bf16[4096,512]{1,0:T(8,128)(2,1)} async-done(((bf16[256,512]{1,0:T(8,128)(2,1)}), bf16[4096,512]{1,0:T(8,128)(2,1)}) %all-gather.13.cloned.1.call-update) | async-done | bytes 4194320 | tf_op jit(solution)/shard_map/all_gather | solution.py:221
  774.6 36.1 %reduce-scatter.8.cloned.1.call-done = bf16[256,512]{1,0:T(8,128)(2,1)} async-done(((bf16[256,4096]{1,0:T(8,128)(2,1)}), bf16[256,512]{1,0:T(8,128)(2,1)}) %reduce-scatter.8.cloned.1.call-update) | async-done | bytes 262160 | tf_op jit(solution)/shard_map/reduce_scatter | solution.py:228
  810.7 6.3 fusion.34
  (274 shorter events, 140.0 us)
Async XLA Ops:
  7.2 1.7 copy-start
  7.2 104.4 %reduce-scatter.4.cloned.1.call-start = ((), (), s32[]{:S(2)}) async-start(), calls=%async_computation.5 | async-start | bytes 4456448 | tf_op jit(solution)/shard_map/reduce_scatter | solution.py:114
  31.4 80.2 %copy-start.28 = (s32[128]{0:T(128)S(1)}, s32[128]{0:T(128)}, u32[]{:S(2)}) copy-start(s32[128]{0:T(128)} %param.41) | copy-start | bytes 1540
  31.4 80.6 %copy-start.6 = (f32[16,8,4096]{2,1,0:T(8,128)S(1)}, f32[16,8,4096]{2,1,0:T(8,128)}, u32[]{:S(2)}) copy-start(f32[16,8,4096]{2,1,0:T(8,128)} %param.40) | copy-start | bytes 6291460
  31.4 81.3 %copy-start.26 = (s32[16]{0:T(128)S(1)}, s32[16]{0:T(128)}, u32[]{:S(2)}) copy-start(s32[16]{0:T(128)} %param.43) | copy-start | bytes 196
  31.5 89.0 %copy-start.20 = (f32[3,4096]{1,0:T(4,128)S(1)}, f32[3,4096]{1,0:T(4,128)}, u32[]{:S(2)}) copy-start(f32[3,4096]{1,0:T(4,128)} %param.29) | copy-start | bytes 147460
  31.5 89.0 %copy-start.16 = (bf16[16,512]{1,0:T(8,128)(2,1)S(1)}, bf16[16,512]{1,0:T(8,128)(2,1)}, u32[]{:S(2)}) copy-start(bf16[16,512]{1,0:T(8,128)(2,1)} %param.27) | copy-start | bytes 49156
  31.5 148.8 %all-gather.7.cloned.1.call-start = ((), (), s32[]{:S(2)}) async-start(), calls=%async_computation.6 | async-start | bytes 2359296 | tf_op jit(solution)/shard_map/all_gather | solution.py:121
  111.9 628.2 %copy-start.22 = (pred[16]{0:T(512)(128)(4,1)}, pred[16]{0:T(512)(128)(4,1)S(1)}, u32[]{:S(2)}) copy-start(pred[16]{0:T(512)(128)(4,1)S(1)} %get-tuple-element.137) | copy-start | bytes 52
  114.6 51.6 %all-to-all-start = ((bf16[16,8,4096]{2,1,0:T(8,128)(2,1)}), bf16[16,8,4096]{2,1,0:T(8,128)(2,1)}, u32[]{:S(2)}, u32[]{:S(2)}) async-start(bf16[16,8,4096]{2,1,0:T(8,128)(2,1)} %select_convert_fusion.1), calls=%async_computation.1 | async-start | bytes 2097152 | tf_op jit(solution)/shard_map/all_to_all | solution.py:162
  119.6 384.4 %all-gather.9.cloned.1.call-start = ((), (), s32[]{:S(2)}) async-start(), calls=%async_computation.7 | async-start | bytes 4456448 | tf_op jit(solution)/shard_map/all_gather | solution.py:204
  120.4 427.8 %reduce-scatter.6.cloned.1.call-start = ((), (), s32[]{:S(2)}) async-start(), calls=%async_computation.8 | async-start | bytes 2359296 | tf_op jit(solution)/shard_map/reduce_scatter | solution.py:207
  120.5 597.6 %copy-start.13 = (f32[1,4096]{1,0:T(1,128)}, f32[1,4096]{1,0:T(1,128)S(1)}, u32[]{:S(2)}) copy-start(f32[1,4096]{1,0:T(1,128)S(1)} %get-tuple-element.155) | copy-start | bytes 49156
  156.8 6.5 copy-start.23
  156.8 8.7 %copy-start.15 = (f32[7,4096]{1,0:T(8,128)S(1)}, f32[7,4096]{1,0:T(8,128)}, u32[]{:S(2)}) copy-start(f32[7,4096]{1,0:T(8,128)} %param.30) | copy-start | bytes 344068
  180.3 4.6 copy-start.2
  182.4 3.3 copy-start.11
  185.7 2.0 copy-start.4
  187.7 5.6 copy-start.27
  203.2 6.4 copy-start.8
  203.2 6.4 copy-start.10
  209.6 3.4 copy-start.7
  209.6 3.4 copy-start.9
  513.3 39.0 %copy-start.18 = (bf16[16,512]{1,0:T(8,128)(2,1)S(1)}, bf16[16,512]{1,0:T(8,128)(2,1)}, u32[]{:S(2)}) copy-start(bf16[16,512]{1,0:T(8,128)(2,1)} %param.28) | copy-start | bytes 49156
  513.3 61.3 %all-gather.11.cloned.1.call-start = ((), (), s32[]{:S(2)}) async-start(), calls=%async_computation.9 | async-start | bytes 2359296 | tf_op jit(solution)/shard_map/all_gather | solution.py:212
  550.1 93.0 %all-gather.15.cloned.1.call-start = ((), (), s32[]{:S(2)}) async-start(), calls=%async_computation.11 | async-start | bytes 7798784 | tf_op jit(solution)/shard_map/all_gather | solution.py:220
  550.7 167.4 %all-gather.17.cloned.1.call-start = ((), (), s32[]{:S(2)}) async-start(), calls=%async_computation.12 | async-start | bytes 7798784 | tf_op jit(solution)/shard_map/all_gather | solution.py:225
  551.4 223.2 %all-gather.13.cloned.1.call-start = ((), (), s32[]{:S(2)}) async-start(), calls=%async_computation.10 | async-start | bytes 4456448 | tf_op jit(solution)/shard_map/all_gather | solution.py:221
  552.2 258.5 %reduce-scatter.8.cloned.1.call-start = ((), (), s32[]{:S(2)}) async-start(), calls=%async_computation.13 | async-start | bytes 2359296 | tf_op jit(solution)/shard_map/reduce_scatter | solution.py:228
  574.6 4.4 copy-start.3
  579.9 2.1 copy-start.5
  734.9 21.6 %all-to-all-start.1 = ((bf16[16,8,4096]{2,1,0:T(8,128)(2,1)}), bf16[16,8,4096]{2,1,0:T(8,128)(2,1)S(1)}, u32[]{:S(2)}, u32[]{:S(2)}) async-start(bf16[16,8,4096]{2,1,0:T(8,128)(2,1)} %fusion.17), calls=%async_computation.4 | async-start | bytes 2097152 | tf_op jit(solution)/shard_map/all_to_all | solution.py:253
  756.6 54.1 %copy-start.12 = (bf16[256,512]{1,0:T(8,128)(2,1)S(1)}, bf16[256,512]{1,0:T(8,128)(2,1)}, u32[]{:S(2)}) copy-start(bf16[256,512]{1,0:T(8,128)(2,1)} %add_convert_fusion.39) | copy-start | bytes 786436
  760.5 4.3 copy-start.17
  760.5 4.3 copy-start.19
  760.6 4.3 copy-start.24
  760.6 4.3 copy-start.25
  760.6 50.1 %copy-start.14 = (f32[1,4096]{1,0:T(1,128)S(1)}, f32[1,4096]{1,0:T(1,128)}, u32[]{:S(2)}) copy-start(f32[1,4096]{1,0:T(1,128)} %copy-done.13) | copy-start | bytes 49156
  760.6 50.1 %copy-start.21 = (f32[1,4096]{1,0:T(1,128)S(1)}, f32[1,4096]{1,0:T(1,128)}, u32[]{:S(2)}) copy-start(f32[1,4096]{1,0:T(1,128)} %get-tuple-element.154) | copy-start | bytes 49156
  810.7 6.3 copy-start.1
Sparse Core Ops, SparseCore 0:
  31.6 79.9 reduce-scatter.3
  113.4 24.9 all-gather.6
  140.7 57.6 all-gather.8
  513.4 34.7 reduce-scatter.5
  550.4 24.1 all-gather.10
  576.8 66.2 all-gather.14
  645.5 72.5 all-gather.16
  720.5 54.0 all-gather.12
  777.1 33.5 reduce-scatter.7
where the time goes:
time: 836 us; the launch traced here: 824 us
  waiting for transfers between devices  314 us (38%)
  other arithmetic  176 us (21%)
  local copies, waits for them, and re-layouts  136 us (16%)
  matrix products  135 us (16%)
  blocking collectives  26 us (3%)
  between operations  14.7 us (2%)
  loops' own time  11 us (1%)
  starting transfers between devices  10.5 us (1%)
    select_n x16, other arithmetic, scan_step(): jnp.where((accepted_count == step_index + 1)[:, None, None, None], wkv_st...  105 us
    dot_general x16, matrix products, scan_step(): jnp.einsum('bhi,bhij->bhj', current_receptance, wkv_state, precision=lax....  84.5 us
    reduce_scatter x1, waiting for transfers between devices, body(): lax.psum_scatter(jnp.where(inside[:, None], found.astype(jnp.float32), 0....  80 us
    all_gather x1, waiting for transfers between devices, body(): lax.all_gather(feedforward_content_matrix, 'tok', axis=1, tiled=True)  75 us
    all_gather x1, waiting for transfers between devices, body(): lax.all_gather(feedforward_lookup_matrix, 'tok', axis=0, tiled=True)  58 us
    dynamic_slice x48, local copies, waits for them, and re-layouts, memory_matrix_sweep(): lax.scan(scan_step, (initial_memory_matrix, initial_memory_matrix), (gati...  47.6 us
    reduce_scatter x1, waiting for transfers between devices, body(): lax.psum_scatter(partial_ffn.astype(jnp.bfloat16), 'grp', scatter_dimensi...  36.1 us
    reduce_scatter x1, waiting for transfers between devices, body(): lax.psum_scatter(partial_att.astype(jnp.bfloat16), 'grp', scatter_dimensi...  30.8 us
  transfers between devices with their start and end apart: 11, of which 8 were waited for; matrix products, arithmetic and copies ran while one was open for 49% of the time, Pallas kernels for 0%

commit v1 on v0

--- a/solution.py
+++ b/solution.py
@@ -8,6 +8,11 @@
 GUESS_SYMBOLS = 16
 EPSILON = 1e-05
 HEAD_EPSILON = 0.00064
+
+
+def gather_from_all(value, axis, dim):
+    copies = jnp.concatenate([value] * lax.axis_size(axis), axis=dim)
+    return lax.all_to_all(copies, axis, dim, dim, tiled=True)
 
 
 def normalize(tensor, gain_row, eps_value):
@@ -222,7 +227,7 @@
     hidden = jnp.square(jax.nn.relu(key_sum)).astype(jnp.bfloat16)
     partial_ffn = jnp.dot(
         hidden,
-        lax.all_gather(feedforward_content_matrix, "tok", axis=1, tiled=True),
+        gather_from_all(feedforward_content_matrix, "tok", 1),
         preferred_element_type=jnp.float32,
     )
     ffn_share = lax.psum_scatter(

time: 836 us -> 844 us (level)
  waiting for transfers between devices: 314 us -> 284 us
  local copies, waits for them, and re-layouts: 136 us -> 162 us
  starting transfers between devices: 10.5 us -> 21.7 us
    all_to_all x0 -> x1, waiting for transfers between devices: none -> 107 us  [gather_from_all(): return lax.all_to_all(copies, axis, dim, dim, tiled=True)]
    all_gather x1 -> x0, waiting for transfers between devices: 75 us -> none  [body(): lax.all_gather(feedforward_content_matrix, 'tok', axis=1, tiled=True)]
    all_gather x1, waiting for transfers between devices: 58 us -> 0.01 us  [body(): lax.all_gather(feedforward_lookup_matrix, 'tok', axis=0, tiled=True)]
    all_to_all x0 -> x2, local copies, waits for them, and re-layouts: none -> 22.7 us  [gather_from_all(): return lax.all_to_all(copies, axis, dim, dim, tiled=True)]
    all_gather x1, waiting for transfers between devices: 9.24 us -> 0.01 us  [body(): whole_res = lax.all_gather(residual, 'grp', axis=1, tiled=True)]
  transfers between devices with their start and end apart: 11 -> 11, of which waited for: 8 -> 6; matrix products, arithmetic and copies ran while one was open for 49% -> 51% of each run, Pallas kernels for 0% -> 0%
where the time goes in v1:
time: 844 us; the launch traced here: 831 us
  waiting for transfers between devices  284 us (34%)
  other arithmetic  175 us (21%)
  local copies, waits for them, and re-layouts  162 us (19%)
  matrix products  136 us (16%)
  blocking collectives  26 us (3%)
  starting transfers between devices  21.7 us (3%)
  between operations  15.4 us (2%)
  loops' own time  11 us (1%)
    all_to_all x1, waiting for transfers between devices, gather_from_all(): return lax.all_to_all(copies, axis, dim, dim, tiled=True)  107 us
    select_n x16, other arithmetic, scan_step(): jnp.where((accepted_count == step_index + 1)[:, None, None, None], wkv_st...  106 us
    dot_general x16, matrix products, scan_step(): jnp.einsum('bhi,bhij->bhj', current_receptance, wkv_state, precision=lax....  84.5 us
    reduce_scatter x1, waiting for transfers between devices, body(): lax.psum_scatter(jnp.where(inside[:, None], found.astype(jnp.float32), 0....  80 us
    dynamic_slice x48, local copies, waits for them, and re-layouts, memory_matrix_sweep(): lax.scan(scan_step, (initial_memory_matrix, initial_memory_matrix), (gati...  47.6 us
    reduce_scatter x1, waiting for transfers between devices, body(): lax.psum_scatter(partial_ffn.astype(jnp.bfloat16), 'grp', scatter_dimensi...  42.4 us
    reduce_scatter x1, waiting for transfers between devices, body(): lax.psum_scatter(partial_att.astype(jnp.bfloat16), 'grp', scatter_dimensi...  32.3 us
    dot_general x4, local copies, waits for them, and re-layouts, project(): jnp.dot(mix_input(normed, before, lagged_blend_ratios[index]), weight, pr...  28.6 us
  transfers between devices with their start and end apart: 11, of which 6 were waited for; matrix products, arithmetic and copies ran while one was open for 51% of the time, Pallas kernels for 0%

profile of v1, /device:TPU:0, one launch (start us, length us, event | category | flops | bytes accessed | tf_op | source)
XLA Modules:
  0.0 830.6 jit_solution(6288199194279519438)
XLA Ops:
  8.9 17.3 %gather_fusion = bf16[4096,512]{1,0:T(8,128)(2,1)} fusion(bf16[2048,512]{1,0:T(8,128)(2,1)S(1)} %copy-done, s32[4096]{0:T(1024)S(1)} %fusion.51), kind=kCustom, calls=%fused_computation.4 | custom fusion | bytes 8404992 | tf_op jit(solution)/shard_map/jit(_take)/gather | solution.py:118
  26.2 5.3 select_convert_fusion
  31.6 80.0 %reduce-scatter.4.cloned.1.call-done = bf16[256,512]{1,0:T(8,128)(2,1)} async-done(((bf16[4096,512]{1,0:T(8,128)(2,1)}), bf16[256,512]{1,0:T(8,128)(2,1)}) %reduce-scatter.4.cloned.1.call-update) | async-done | bytes 262160 | tf_op jit(solution)/shard_map/reduce_scatter | solution.py:119
  114.6 5.0 all-to-all-start
  120.6 13.3 %all_gather.22 = bf16[16,4096]{1,0:T(8,128)(2,1)S(1)} all-gather(bf16[16,512]{1,0:T(8,128)(2,1)S(1)} %copy-done.21), channel_id=1, replica_groups=mesh['grp'=8,'tok'=16] {'grp'}, dimensions={1}, use_global_device_ids=true | all-gather | bytes 147456 | tf_op jit(solution)/shard_map/all_gather | solution.py:127
  134.7 9.1 %slice_bitcast_fusion = (bf16[512,4096]{0,1:T(8,128)(2,1)}, bf16[512,4096]{0,1:T(8,128)(2,1)}, bf16[512,4096]{0,1:T(8,128)(2,1)}) fusion(bf16[4,4096,512]{2,1,0:T(8,128)(2,1)} %param.31), kind=kLoop, calls=%fused_computation.44 | loop fusion | bytes 25165824 | tf_op jit(solution)/shard_map/dot_general | solution.py:137
  143.9 6.4 copy.87
  150.3 6.4 copy.86
  156.7 6.6 copy.85
  174.6 3.0 reshape.317
  187.7 5.3 add_convert_fusion.3
  193.1 5.3 fusion.29
  203.0 6.3 convolution_bitcast_fusion
  209.3 3.3 convolution_bitcast_fusion.1
  212.7 3.3 convolution_bitcast_fusion.2
  216.0 285.4 %while.14 = (s32[]{:T(128)}, f32[16,8,64,64]{3,2,1,0:T(8,128)}, bf16[16,8,64,64]{3,2,1,0:T(8,128)(2,1)S(1)}, f32[16,16,8,64]{3,2,1,0:T(8,128)S(1)}, f32[16,16,8,...) while((s32[]{:T(128)}, f32[16,8,64,64]{3,2,1,0:T(8,128)}, ...), condition=%wide.region_9.11_spmd, body=%wide.region_7.10_spmd.sunk | while | flops 8421586 | bytes 9150729 | solution.py:66
  217.3 5.3 fusion.91
  227.2 6.6 broadcast_select_fusion.5
  235.1 5.3 fusion.91
  245.0 6.6 broadcast_select_fusion.5
  252.9 5.3 fusion.91
  262.9 6.6 broadcast_select_fusion.5
  270.8 5.3 fusion.91
  280.7 6.6 broadcast_select_fusion.5
  288.6 5.3 fusion.91
  298.5 6.6 broadcast_select_fusion.5
  306.4 5.3 fusion.91
  316.3 6.6 broadcast_select_fusion.5
  324.2 5.3 fusion.91
  334.2 6.6 broadcast_select_fusion.5
  342.1 5.3 fusion.91
  352.0 6.6 broadcast_select_fusion.5
  359.9 5.3 fusion.91
  369.8 6.6 broadcast_select_fusion.5
  377.7 5.3 fusion.91
  387.6 6.6 broadcast_select_fusion.5
  395.5 5.3 fusion.91
  405.5 6.6 broadcast_select_fusion.5
  413.4 5.3 fusion.91
  423.3 6.6 broadcast_select_fusion.5
  431.2 5.3 fusion.91
  441.1 6.6 broadcast_select_fusion.5
  449.0 5.3 fusion.91
  458.9 6.6 broadcast_select_fusion.5
  466.8 5.3 fusion.91
  476.8 6.6 broadcast_select_fusion.5
  484.7 5.3 fusion.91
  494.6 6.6 broadcast_select_fusion.5
  504.3 9.4 %convolution_convert_fusion.1 = bf16[256,4096]{1,0:T(8,128)(2,1)} fusion(bf16[512,4096]{1,0:T(8,128)(2,1)} %all-gather.8.cloned.1.call-done, f32[256,512]{1,0:T(8,128)} %reshape.320, bf16[4,4096,512]{2,1,0:T(8,128)(2,1)} %param.31, f32[256,4096]{1,0:T(8,128)} %get-tuple-element.175, f32[4096]{0:T(1024)S(1)} %bitcast.229, ...), kind=kOutput, calls=%fused_computation.28 | convolution fusion | flops 2156658688 | bytes 17336320 | tf_op jit(solution)/shard_map/dot_general | solution.py:207
  516.3 32.3 %reduce-scatter.6.cloned.1.call-done = bf16[256,512]{1,0:T(8,128)(2,1)} async-done(((bf16[256,4096]{1,0:T(8,128)(2,1)}), bf16[256,512]{1,0:T(8,128)(2,1)}) %reduce-scatter.6.cloned.1.call-update) | async-done | bytes 262160 | tf_op jit(solution)/shard_map/reduce_scatter | solution.py:212
  552.3 2.9 copy-done.9
  555.2 11.2 %copy.108 = bf16[896,16,256]{2,0,1:T(8,128)(2,1)} copy(bf16[896,16,256]{0,2,1:T(8,128)(2,1)} %bitcast.203) | data formatting | bytes 14680064 | tf_op jit(solution)/shard_map/all_to_all | solution.py:15
  566.4 7.0 all-to-all-start.1
  574.3 12.8 %all_gather.25 = bf16[16,4096]{1,0:T(8,128)(2,1)S(1)} all-gather(bf16[16,512]{1,0:T(8,128)(2,1)S(1)} %copy-done.23), channel_id=1, replica_groups=mesh['grp'=8,'tok'=16] {'grp'}, dimensions={1}, use_global_device_ids=true | all-gather | bytes 147456 | tf_op jit(solution)/shard_map/all_gather | solution.py:128
  587.4 106.9 %all-to-all-done.1 = bf16[896,16,256]{2,0,1:T(8,128)(2,1)} async-done(((bf16[896,16,256]{2,0,1:T(8,128)(2,1)}), bf16[896,16,256]{2,0,1:T(8,128)(2,1)}, u32[]{:S(2)}, u32[]{:S(2)}) %all-to-all-start.1) | async-done | bytes 7340064 | tf_op jit(solution)/shard_map/all_to_all | solution.py:15
  694.3 11.5 %copy.109 = bf16[896,16,256]{0,2,1:T(8,128)(2,1)} copy(bf16[896,16,256]{2,0,1:T(8,128)(2,1)} %all-to-all-done.1) | data formatting | bytes 14680064 | tf_op jit(solution)/shard_map/all_to_all | solution.py:15
  712.9 3.1 bitcast_subtract_fusion
  716.1 13.1 %convolution_convert_fusion = bf16[256,4096]{1,0:T(8,128)(2,1)} fusion(bf16[896,4096]{0,1:T(8,128)(2,1)} %bitcast.204, bf16[4096,896]{1,0:T(8,128)(2,1)} %all-gather.14.cloned.1.call-done, f32[256,4096]{1,0:T(8,128)} %bitcast_subtract_fusion, f32[4096]{0:T(1024)S(1)} %bitcast.228, bf16[256,4096]{1,0:T(8,128)(2,1)} %all-gather.10.cloned.1.call-done, ...), kind=kOutput, calls=%fused_computation.27 | convolution fusion | flops 3767173120 | bytes 23103488 | tf_op jit(solution)/shard_map/dot_general | solution.py:228
  733.1 9.4 %all-to-all-start.2 = ((bf16[16,8,4096]{2,1,0:T(8,128)(2,1)}), bf16[16,8,4096]{2,1,0:T(8,128)(2,1)S(1)}, u32[]{:S(2)}, u32[]{:S(2)}) async-start(bf16[16,8,4096]{2,1,0:T(8,128)(2,1)} %fusion.17), calls=%async_computation.5 | async-start | bytes 2097152 | tf_op jit(solution)/shard_map/all_to_all | solution.py:258
  745.4 10.4 %all-to-all-done.2 = bf16[16,8,4096]{2,1,0:T(8,128)(2,1)S(1)} async-done(((bf16[16,8,4096]{2,1,0:T(8,128)(2,1)}), bf16[16,8,4096]{2,1,0:T(8,128)(2,1)S(1)}, u32[]{:S(2)}, u32[]{:S(2)}) %all-to-all-start.2) | async-done | bytes 1048608 | tf_op jit(solution)/shard_map/all_to_all | solution.py:258
  755.8 4.0 convolution_select_fusion
  764.7 9.8 %all-gather.12.cloned.1.call-done = bf16[4096,512]{1,0:T(8,128)(2,1)} async-done(((bf16[256,512]{1,0:T(8,128)(2,1)}), bf16[4096,512]{1,0:T(8,128)(2,1)}) %all-gather.12.cloned.1.call-update) | async-done | bytes 4194320 | tf_op jit(solution)/shard_map/all_gather | solution.py:226
  774.5 42.4 %reduce-scatter.8.cloned.1.call-done = bf16[256,512]{1,0:T(8,128)(2,1)} async-done(((bf16[256,4096]{1,0:T(8,128)(2,1)}), bf16[256,512]{1,0:T(8,128)(2,1)}) %reduce-scatter.8.cloned.1.call-update) | async-done | bytes 262160 | tf_op jit(solution)/shard_map/reduce_scatter | solution.py:233
  816.9 6.3 fusion.34
  (300 shorter events, 145.3 us)
Async XLA Ops:
  7.2 1.7 copy-start
  7.2 104.4 %reduce-scatter.4.cloned.1.call-start = ((), (), s32[]{:S(2)}) async-start(), calls=%async_computation.6 | async-start | bytes 4456448 | tf_op jit(solution)/shard_map/reduce_scatter | solution.py:119
  31.5 80.2 %copy-start.33 = (s32[128]{0:T(128)S(1)}, s32[128]{0:T(128)}, u32[]{:S(2)}) copy-start(s32[128]{0:T(128)} %param.41) | copy-start | bytes 1540
  31.5 80.6 %copy-start.10 = (f32[16,8,4096]{2,1,0:T(8,128)S(1)}, f32[16,8,4096]{2,1,0:T(8,128)}, u32[]{:S(2)}) copy-start(f32[16,8,4096]{2,1,0:T(8,128)} %param.40) | copy-start | bytes 6291460
  31.5 81.3 %copy-start.31 = (s32[16]{0:T(128)S(1)}, s32[16]{0:T(128)}, u32[]{:S(2)}) copy-start(s32[16]{0:T(128)} %param.43) | copy-start | bytes 196
  31.5 89.0 %copy-start.25 = (f32[3,4096]{1,0:T(4,128)S(1)}, f32[3,4096]{1,0:T(4,128)}, u32[]{:S(2)}) copy-start(f32[3,4096]{1,0:T(4,128)} %param.29) | copy-start | bytes 147460
  31.5 89.0 %copy-start.21 = (bf16[16,512]{1,0:T(8,128)(2,1)S(1)}, bf16[16,512]{1,0:T(8,128)(2,1)}, u32[]{:S(2)}) copy-start(bf16[16,512]{1,0:T(8,128)(2,1)} %param.27) | copy-start | bytes 49156
  31.5 148.8 %all-gather.6.cloned.1.call-start = ((), (), s32[]{:S(2)}) async-start(), calls=%async_computation.7 | async-start | bytes 2359296 | tf_op jit(solution)/shard_map/all_gather | solution.py:126
  111.9 630.6 %copy-start.27 = (pred[16]{0:T(512)(128)(4,1)}, pred[16]{0:T(512)(128)(4,1)S(1)}, u32[]{:S(2)}) copy-start(pred[16]{0:T(512)(128)(4,1)S(1)} %get-tuple-element.167) | copy-start | bytes 52
  114.6 51.6 %all-to-all-start = ((bf16[16,8,4096]{2,1,0:T(8,128)(2,1)}), bf16[16,8,4096]{2,1,0:T(8,128)(2,1)}, u32[]{:S(2)}, u32[]{:S(2)}) async-start(bf16[16,8,4096]{2,1,0:T(8,128)(2,1)} %select_convert_fusion.1), calls=%async_computation.1 | async-start | bytes 2097152 | tf_op jit(solution)/shard_map/all_to_all | solution.py:167
  119.6 384.7 %all-gather.8.cloned.1.call-start = ((), (), s32[]{:S(2)}) async-start(), calls=%async_computation.8 | async-start | bytes 4456448 | tf_op jit(solution)/shard_map/all_gather | solution.py:209
  120.4 428.2 %reduce-scatter.6.cloned.1.call-start = ((), (), s32[]{:S(2)}) async-start(), calls=%async_computation.9 | async-start | bytes 2359296 | tf_op jit(solution)/shard_map/reduce_scatter | solution.py:212
  120.5 595.5 %copy-start.18 = (f32[1,4096]{1,0:T(1,128)}, f32[1,4096]{1,0:T(1,128)S(1)}, u32[]{:S(2)}) copy-start(f32[1,4096]{1,0:T(1,128)S(1)} %get-tuple-element.185) | copy-start | bytes 49156
  156.7 6.6 copy-start.28
  156.7 8.8 %copy-start.20 = (f32[7,4096]{1,0:T(8,128)S(1)}, f32[7,4096]{1,0:T(8,128)}, u32[]{:S(2)}) copy-start(f32[7,4096]{1,0:T(8,128)} %param.30) | copy-start | bytes 344068
  180.3 4.6 copy-start.4
  182.4 3.3 copy-start.15
  185.7 2.0 copy-start.7
  187.7 5.3 copy-start.32
  203.0 6.3 copy-start.12
  203.0 6.3 copy-start.14
  209.3 3.3 copy-start.11
  209.3 3.3 copy-start.13
  501.4 2.9 copy-start.2
  504.3 9.5 %copy-start.5 = (bf16[256,4096]{1,0:T(8,128)(2,1)S(1)}, bf16[256,4096]{1,0:T(8,128)(2,1)}, u32[]{:S(2)}) copy-start(bf16[256,4096]{1,0:T(8,128)(2,1)} %all-gather.6.cloned.1.call-done) | copy-start | bytes 6291460
  513.7 37.4 %copy-start.17 = (bf16[896,256]{1,0:T(8,128)(2,1)S(1)}, bf16[896,256]{1,0:T(8,128)(2,1)}, u32[]{:S(2)}) copy-start(bf16[896,256]{1,0:T(8,128)(2,1)} %param.38) | copy-start | bytes 1376260
  513.8 192.0 %all-gather.10.cloned.1.call-start = ((), (), s32[]{:S(2)}) async-start(), calls=%async_computation.10 | async-start | bytes 2359296 | tf_op jit(solution)/shard_map/all_gather | solution.py:217
  550.5 165.6 %all-gather.14.cloned.1.call-start = ((), (), s32[]{:S(2)}) async-start(), calls=%async_computation.12 | async-start | bytes 7798784 | tf_op jit(solution)/shard_map/all_gather | solution.py:225
  552.3 2.9 copy-start.9
  566.4 7.8 copy-start.23
  566.4 127.9 %all-to-all-start.1 = ((bf16[896,16,256]{2,0,1:T(8,128)(2,1)}), bf16[896,16,256]{2,0,1:T(8,128)(2,1)}, u32[]{:S(2)}, u32[]{:S(2)}) async-start(bf16[896,16,256]{2,0,1:T(8,128)(2,1)} %copy.108), calls=%async_computation.3 | async-start | bytes 14680064 | tf_op jit(solution)/shard_map/all_to_all | solution.py:15
  573.5 201.0 %all-gather.12.cloned.1.call-start = ((), (), s32[]{:S(2)}) async-start(), calls=%async_computation.11 | async-start | bytes 4456448 | tf_op jit(solution)/shard_map/all_gather | solution.py:226
  574.2 242.7 %reduce-scatter.8.cloned.1.call-start = ((), (), s32[]{:S(2)}) async-start(), calls=%async_computation.13 | async-start | bytes 2359296 | tf_op jit(solution)/shard_map/reduce_scatter | solution.py:233
  705.8 4.4 copy-start.6
  711.0 1.9 copy-start.8
  716.1 13.3 %copy-start.3 = (bf16[16,8,64,64]{3,2,1,0:T(8,128)(2,1)S(1)}, bf16[16,8,64,64]{3,2,1,0:T(8,128)(2,1)}, u32[]{:S(2)}) copy-start(bf16[16,8,64,64]{3,2,1,0:T(8,128)(2,1)} %copy-done.2) | copy-start | bytes 3145732
  733.1 22.7 %all-to-all-start.2 = ((bf16[16,8,4096]{2,1,0:T(8,128)(2,1)}), bf16[16,8,4096]{2,1,0:T(8,128)(2,1)S(1)}, u32[]{:S(2)}, u32[]{:S(2)}) async-start(bf16[16,8,4096]{2,1,0:T(8,128)(2,1)} %fusion.17), calls=%async_computation.5 | async-start | bytes 2097152 | tf_op jit(solution)/shard_map/all_to_all | solution.py:258
  755.8 61.2 %copy-start.16 = (bf16[256,512]{1,0:T(8,128)(2,1)S(1)}, bf16[256,512]{1,0:T(8,128)(2,1)}, u32[]{:S(2)}) copy-start(bf16[256,512]{1,0:T(8,128)(2,1)} %add_convert_fusion.39) | copy-start | bytes 786436
  759.7 4.3 copy-start.22
  759.8 4.3 copy-start.24
  759.8 4.3 copy-start.29
  759.8 4.3 copy-start.30
  759.8 57.2 %copy-start.19 = (f32[1,4096]{1,0:T(1,128)S(1)}, f32[1,4096]{1,0:T(1,128)}, u32[]{:S(2)}) copy-start(f32[1,4096]{1,0:T(1,128)} %copy-done.18) | copy-start | bytes 49156
  759.8 57.1 %copy-start.26 = (f32[1,4096]{1,0:T(1,128)S(1)}, f32[1,4096]{1,0:T(1,128)}, u32[]{:S(2)}) copy-start(f32[1,4096]{1,0:T(1,128)} %get-tuple-element.184) | copy-start | bytes 49156
  816.9 6.3 copy-start.1
Sparse Core Ops, SparseCore 0:
  31.6 79.9 reduce-scatter.3
  113.4 24.9 all-gather.5
  140.8 57.6 all-gather.7
  513.9 34.6 reduce-scatter.5
  550.8 24.0 all-gather.9
  577.1 134.1 all-gather.13
  713.6 60.8 all-gather.11
  777.0 39.8 reduce-scatter.7
